TPU v7x, 128 devices: a whole 4x4x4 slice. The times are simulated.
128 devices in a mesh: seq: 32 (over x, y, core), tp: 4 (over z).
Axes of the slice: x: 4, y: 4, z: 4, core: 2. Of those that a mesh axis runs over, the one named last changes fastest.
Arguments:
- tokens: bfloat16 [49152, 1792], P('seq', 'tp'), may hold values from -8 to 8
- w_query: bfloat16 [1792, 256], P('seq', 'tp'), may hold values from -0.125 to 0.125
- w_key: bfloat16 [1792, 256], P('seq', 'tp'), may hold values from -0.125 to 0.125
- w_value: bfloat16 [1792, 1792], P('seq', 'tp'), may hold values from -0.125 to 0.125
- prompt_lengths: int32 [32], replicated, may hold values from 1 to 24576, as said below
- owner_slot: int32 [32], replicated, may hold values from 0 to 31, each once
- resume_flag: int32 [32], replicated, may hold values 0 or 1
- init_state: float32 [32, 273, 1792], P('seq', None, 'tp'), may hold values from -0.5 to 0.5
- init_norm: float32 [32, 273, 16], P('seq', None, 'tp'), may hold values from -0.5 to 0.5, as said below
Outputs:
- heads_out: bfloat16 [49152, 1792], P('seq', 'tp')
- final_state: float32 [32, 273, 1792], P('seq', None, 'tp')
- final_norm: float32 [32, 273, 16], P('seq', None, 'tp')
Inputs may be any that keep to these rules, and one draw needn't show every extreme that they name: `prompt_lengths`: prompt r takes the packed positions after those of prompts 0 to r - 1; the lengths sum to 49152; the longest prompt starts and ends at multiples of 1536; every block of 1536 positions that it does not cover holds the end of at least one prompt; no block holds the ends of more than 4 prompts, and one holds exactly 4. `owner_slot`: every row of the state arrays belongs to exactly one request. `resume_flag`: 1 where the request continues from its given states, 0 where it is new. `init_norm`: for every request and head, the inner product with phi(u) is at least half of the row's first entry, and that entry is positive, for every u.
All inputs are finite; a program needn't handle non-finite values.
Results may differ from a plain program's by a relative error of at most 0.0041.
Values may be sent and summed in bfloat16 or wider, within the bound.
A program may use at most 192 MiB of HBM per device.

v0:
```python
import math

import jax
import jax.numpy as jnp
from jax import lax
from jax.sharding import PartitionSpec as P

FD = 16
END_SLOTS = 4


full_precision = lax.Precision.HIGHEST


def carried_in(value, axis, join, neutral):
    count, mine = (lax.axis_size(axis), lax.axis_index(axis))
    pieces = jax.tree.map(lambda part: lax.all_gather(part, axis), value)
    total = jax.tree.map(
        lambda part, zero: jnp.full_like(part, 0) + jnp.asarray(zero, part.dtype), value, neutral
    )

    def hop(position, total):
        longer = join(total, jax.tree.map(lambda part: part[position], pieces))
        return jax.tree.map(lambda new, old: jnp.where(position < mine, new, old), longer, total)

    return lax.fori_loop(0, count - 1, hop, total)


def feature_map(vectors):
    feat_dim = vectors.shape[-1]
    second = (vectors[..., :, None] * vectors[..., None, :]).reshape(
        vectors.shape[:-1] + (feat_dim * feat_dim,)
    )
    unit_column = jnp.ones(vectors.shape[:-1] + (1,), vectors.dtype)
    return jnp.concatenate(
        [unit_column, vectors / feat_dim**0.25, second / math.sqrt(2.0 * feat_dim)], axis=-1
    )


def lookup(table, indices, request_range):
    return jnp.sum(jnp.where(indices[..., None] == request_range, table, 0), axis=-1)


def local(
    tokens, w_query, w_key, w_value, prompt_lengths, owner_slot, resume_flag, init_state, init_norm
):
    gathered = lax.all_gather(tokens, "tp", axis=1, tiled=True)
    tok_rows = gathered.shape[0]
    head_count = w_query.shape[1] // FD
    value_width = w_value.shape[1] // head_count
    state_cols = head_count * value_width
    feat_count = init_state.shape[1]
    req_count = prompt_lengths.shape[0]
    own_count = init_state.shape[0]
    seq_devices = lax.axis_size("seq")
    slot_count = END_SLOTS + 1
    scale_state = 1.0 / (tok_rows * seq_devices // 2)
    pieces = (
        lax.all_gather(w_query, "seq", axis=0, tiled=True),
        lax.all_gather(w_key, "seq", axis=0, tiled=True),
        lax.all_gather(w_value, "seq", axis=0, tiled=True),
    )
    query_sum, key_sum, value_sum = tuple(
        (jnp.dot(gathered, piece, preferred_element_type=jnp.float32) for piece in pieces)
    )
    query_proj = query_sum.astype(jnp.bfloat16).reshape(tok_rows, head_count, FD)
    key_proj = key_sum.astype(jnp.bfloat16).reshape(tok_rows, head_count, FD)
    value_proj = value_sum.astype(jnp.bfloat16)
    value_heads = value_proj.reshape(tok_rows, head_count, value_width)
    seq_index = lax.axis_index("seq")
    first_pos = seq_index * tok_rows
    positions = first_pos + jnp.arange(tok_rows, dtype=jnp.int32)
    end_offsets = jnp.cumsum(prompt_lengths)
    start_offsets = end_offsets - prompt_lengths
    request_ids = jnp.sum((end_offsets[None, :] <= positions[:, None]).astype(jnp.int32), axis=1)
    request_range = jnp.arange(req_count, dtype=jnp.int32)
    first_req = request_ids[0]
    last_req = request_ids[-1]
    touch_count = last_req - first_req + 1
    slot_range = jnp.arange(slot_count, dtype=jnp.int32)
    slot_req = first_req + slot_range
    slot_valid = slot_req <= last_req
    slot_safe = jnp.minimum(slot_req, req_count - 1)
    slot_start = lookup(start_offsets, slot_safe, request_range)
    slot_owner = lookup(owner_slot, slot_safe, request_range)
    slot_resume = lookup(resume_flag, slot_safe, request_range)
    slot_begins = slot_valid & (slot_start >= first_pos)
    continues = slot_start[0] < first_pos
    block_rows = min(512, tok_rows)
    block_count = tok_rows // block_rows

    def attend_block(block_index):
        q_start = block_index * block_rows
        block_q = lax.dynamic_slice_in_dim(query_proj, q_start, block_rows, 0)
        block_req = lax.dynamic_slice_in_dim(request_ids, q_start, block_rows, 0)
        block_pos = lax.dynamic_slice_in_dim(positions, q_start, block_rows, 0)
        req_begin = jnp.sum(jnp.where(request_range == block_req[0], start_offsets, 0))
        low_tile = jnp.maximum(req_begin - first_pos, 0) // block_rows

        def add_tile(tile_index, running):
            k_start = tile_index * block_rows
            tile_k = lax.dynamic_slice_in_dim(key_proj, k_start, block_rows, 0)
            tile_v = lax.dynamic_slice_in_dim(value_heads, k_start, block_rows, 0)
            tile_req = lax.dynamic_slice_in_dim(request_ids, k_start, block_rows, 0)
            tile_pos = lax.dynamic_slice_in_dim(positions, k_start, block_rows, 0)
            scores = jnp.einsum(
                "qhd,khd->hqk", block_q, tile_k, preferred_element_type=jnp.float32
            ) / math.sqrt(FD)
            allowed = (tile_pos[None, :] <= block_pos[:, None]) & (
                tile_req[None, :] == block_req[:, None]
            )
            weight = jnp.where(allowed[None], 1.0 + scores + 0.5 * scores * scores, 0.0).astype(
                jnp.bfloat16
            )
            tile_num = running[0] + jnp.einsum(
                "hqk,khj->qhj", weight, tile_v, preferred_element_type=jnp.float32
            )
            tile_den = running[1] + jnp.sum(weight.astype(jnp.float32), axis=2).T
            return (tile_num, tile_den)

        empty_block = (
            jnp.zeros((block_rows, head_count, value_width), jnp.float32),
            jnp.zeros((block_rows, head_count), jnp.float32),
        )
        return lax.fori_loop(low_tile, block_index + 1, add_tile, empty_block)

    block_num, block_den = lax.map(attend_block, jnp.arange(block_count, dtype=jnp.int32))
    local_num = block_num.reshape(tok_rows, head_count, value_width)
    local_den = block_den.reshape(tok_rows, head_count)
    phi_q = feature_map(query_proj.astype(jnp.float32))
    phi_k = feature_map(key_proj.astype(jnp.float32))
    value_f = value_heads.astype(jnp.float32)

    def slot_terms(slot_index, buffers):
        chosen = (request_ids == first_req + slot_index).astype(jnp.float32)
        weighted = phi_k * chosen[:, None, None]
        state_part = scale_state * jnp.einsum(
            "thf,thj->fhj", weighted, value_f, precision=full_precision
        ).reshape(feat_count, state_cols)
        norm_part = scale_state * jnp.sum(weighted, axis=0).T
        return (
            lax.dynamic_update_index_in_dim(buffers[0], state_part, slot_index, 0),
            lax.dynamic_update_index_in_dim(buffers[1], norm_part, slot_index, 0),
        )

    empty_slots = (
        jnp.zeros((slot_count, feat_count, state_cols), jnp.float32),
        jnp.zeros((slot_count, feat_count, head_count), jnp.float32),
    )
    local_state, local_norm = lax.fori_loop(0, touch_count, slot_terms, empty_slots)
    own_rows = seq_index * own_count + jnp.arange(own_count, dtype=jnp.int32)
    own_resume = jnp.sum(
        jnp.where(owner_slot[None, :] == own_rows[:, None], resume_flag[None, :], 0), axis=1
    ).astype(jnp.float32)
    piece_state = lax.all_gather(init_state, "seq", axis=0, tiled=True)
    piece_norm = lax.all_gather(init_norm, "seq", axis=0, tiled=True)
    row_ids = jnp.arange(piece_state.shape[0], dtype=jnp.int32)
    pick_rows = (
        (slot_owner[:, None] == row_ids[None, :])
        & slot_valid[:, None]
        & (slot_resume[:, None] == 1)
    ).astype(jnp.float32)
    start_state = jnp.einsum("kr,rfc->kfc", pick_rows, piece_state, precision=full_precision)
    start_norm = jnp.einsum("kr,rfh->kfh", pick_rows, piece_norm, precision=full_precision)
    owner_state = own_resume[:, None, None] * init_state
    owner_norm = own_resume[:, None, None] * init_norm
    last_state = lax.dynamic_index_in_dim(local_state, touch_count - 1, 0, keepdims=False)
    last_norm = lax.dynamic_index_in_dim(local_norm, touch_count - 1, 0, keepdims=False)
    starts_here = jnp.any(slot_begins).astype(jnp.float32).reshape(1)

    def combine_carry(earlier, later):
        keep_part = 1.0 - later[0]
        return (
            jnp.maximum(earlier[0], later[0]),
            later[1] + keep_part * earlier[1],
            later[2] + keep_part * earlier[2],
        )

    identity = (jnp.zeros((1,), jnp.float32), jnp.zeros_like(last_state), jnp.zeros_like(last_norm))
    carry_flag, carry_state, carry_norm = carried_in(
        (starts_here, last_state, last_norm), "seq", combine_carry, identity
    )
    first_mask = (slot_range == 0).astype(jnp.float32) * continues.astype(jnp.float32)
    prior_state = start_state + first_mask[:, None, None] * carry_state[None]
    prior_norm = start_norm + first_mask[:, None, None] * carry_norm[None]

    def prior_terms(slot_index, running):
        chosen = (request_ids == first_req + slot_index).astype(jnp.float32)
        slot_state = lax.dynamic_index_in_dim(prior_state, slot_index, 0, keepdims=False).reshape(
            feat_count, head_count, value_width
        )
        slot_norm = lax.dynamic_index_in_dim(prior_norm, slot_index, 0, keepdims=False)
        add_num = jnp.einsum("thf,fhj->thj", phi_q, slot_state, precision=full_precision)
        add_den = jnp.einsum("thf,fh->th", phi_q, slot_norm, precision=full_precision)
        return (
            running[0] + chosen[:, None, None] * add_num,
            running[1] + chosen[:, None] * add_den,
        )

    empty_prior = (
        jnp.zeros((tok_rows, head_count, value_width), jnp.float32),
        jnp.zeros((tok_rows, head_count), jnp.float32),
    )
    prior_num, prior_den = lax.fori_loop(0, touch_count, prior_terms, empty_prior)
    numer = prior_num + scale_state * local_num
    denom = prior_den + scale_state * local_den
    heads_out = (numer / denom[:, :, None]).reshape(tok_rows, state_cols).astype(jnp.bfloat16)
    placement = ((slot_owner[None, :] == request_range[:, None]) & slot_valid[None, :]).astype(
        jnp.float32
    )
    dense_state = jnp.einsum("ok,kfc->ofc", placement, local_state, precision=full_precision)
    dense_norm = jnp.einsum("ok,kfh->ofh", placement, local_norm, precision=full_precision)
    summed_state, summed_norm = (
        lax.psum_scatter(dense_state, "seq", scatter_dimension=0, tiled=True),
        lax.psum_scatter(dense_norm, "seq", scatter_dimension=0, tiled=True),
    )
    final_state = owner_state + summed_state
    final_norm = owner_norm + summed_norm
    return (heads_out, final_state, final_norm)


def solution(mesh):
    in_specs = (
        P("seq", "tp"),
        P("seq", "tp"),
        P("seq", "tp"),
        P("seq", "tp"),
        P(),
        P(),
        P(),
        P("seq", None, "tp"),
        P("seq", None, "tp"),
    )
    out_specs = (P("seq", "tp"), P("seq", None, "tp"), P("seq", None, "tp"))
    return jax.shard_map(local, mesh=mesh, in_specs=in_specs, out_specs=out_specs, check_vma=False)
```

profile of v0, /device:TPU:7, one launch (start us, length us, event | category | flops | bytes accessed | tf_op | source)
XLA Modules:
  0.0 724.2 jit_solution(18156946499815508102)
XLA Ops:
  11.0 25.3 %all_gather.36 = bf16[1792,64]{1,0:T(8,128)(2,1)S(1)} all-gather(bf16[56,64]{1,0:T(8,128)(2,1)} %param.20), channel_id=1, replica_groups=mesh['seq'=32,'tp'=4] {'seq'}, dimensions={0}, use_global_device_ids=true | all-gather | bytes 236544 | tf_op jit(solution)/shard_map/all_gather | solution.py:59
  36.3 22.6 %all_gather.31 = bf16[1792,64]{1,0:T(8,128)(2,1)S(1)} all-gather(bf16[56,64]{1,0:T(8,128)(2,1)} %param.21), channel_id=1, replica_groups=mesh['seq'=32,'tp'=4] {'seq'}, dimensions={0}, use_global_device_ids=true | all-gather | bytes 236544 | tf_op jit(solution)/shard_map/all_gather | solution.py:60
  63.7 7.7 %all-gather.7.cloned.1.call-done = bf16[1536,1792]{0,1:T(8,128)(2,1)} async-done(((bf16[1536,448]{0,1:T(8,128)(2,1)}), bf16[1536,1792]{0,1:T(8,128)(2,1)}) %all-gather.7.cloned.1.call-update) | async-done | bytes 5505040 | tf_op jit(solution)/shard_map/all_gather | solution.py:47
  83.9 33.6 %all-gather.9.cloned.1.call-done = bf16[1792,448]{1,0:T(8,128)(2,1)} async-done(((bf16[56,448]{1,0:T(8,128)(2,1)}), bf16[1792,448]{1,0:T(8,128)(2,1)}) %all-gather.9.cloned.1.call-update) | async-done | bytes 1605648 | tf_op jit(solution)/shard_map/all_gather | solution.py:61
  117.5 6.0 convolution_convert_fusion
  125.3 6.2 pad_maximum_fusion.1
  133.6 72.4 %while.80 = (s32[]{:T(128)}, f32[5,273,448]{2,1,0:T(8,128)}, f32[5,273,4]{1,2,0:T(4,128)S(1)}, s32[]{:T(128)}, s32[]{:T(128)}, /*index=5*/s32[1536]{0:T(1024)S(1...) while((s32[]{:T(128)}, f32[5,273,448]{2,1,0:T(8,128)}, ...), condition=%wide.region_8.9_spmd, body=%wide.region_6.8_spmd.sunk | while | flops 2259464704 | bytes 19721152 | solution.py:150
  134.7 8.8 %fusion.92 = f32[273,4,112]{2,0,1:T(8,128)S(1)} fusion(f32[1536,4,112]{0,2,1:T(8,128)} %get-tuple-element.1145, f32[1536,4,273]{0,2,1:T(8,128)} %get-tuple-element.1144, f32[1536]{0:T(1024)S(1)} %compare_convert_fusion.4), kind=kOutput, calls=%fused_computation.6.clone.1 | convolution fusion | flops 2256107008 | bytes 9957120 | tf_op jit(solution)/shard_map/while/body/thf,thj->fhj/dot_general | solution.py:137
  149.1 8.8 %fusion.92 = f32[273,4,112]{2,0,1:T(8,128)S(1)} fusion(f32[1536,4,112]{0,2,1:T(8,128)} %get-tuple-element.1145, f32[1536,4,273]{0,2,1:T(8,128)} %get-tuple-element.1144, f32[1536]{0:T(1024)S(1)} %compare_convert_fusion.4), kind=kOutput, calls=%fused_computation.6.clone.1 | convolution fusion | flops 2256107008 | bytes 9957120 | tf_op jit(solution)/shard_map/while/body/thf,thj->fhj/dot_general | solution.py:137
  163.5 8.8 %fusion.92 = f32[273,4,112]{2,0,1:T(8,128)S(1)} fusion(f32[1536,4,112]{0,2,1:T(8,128)} %get-tuple-element.1145, f32[1536,4,273]{0,2,1:T(8,128)} %get-tuple-element.1144, f32[1536]{0:T(1024)S(1)} %compare_convert_fusion.4), kind=kOutput, calls=%fused_computation.6.clone.1 | convolution fusion | flops 2256107008 | bytes 9957120 | tf_op jit(solution)/shard_map/while/body/thf,thj->fhj/dot_general | solution.py:137
  177.9 8.8 %fusion.92 = f32[273,4,112]{2,0,1:T(8,128)S(1)} fusion(f32[1536,4,112]{0,2,1:T(8,128)} %get-tuple-element.1145, f32[1536,4,273]{0,2,1:T(8,128)} %get-tuple-element.1144, f32[1536]{0:T(1024)S(1)} %compare_convert_fusion.4), kind=kOutput, calls=%fused_computation.6.clone.1 | convolution fusion | flops 2256107008 | bytes 9957120 | tf_op jit(solution)/shard_map/while/body/thf,thj->fhj/dot_general | solution.py:137
  192.3 8.8 %fusion.92 = f32[273,4,112]{2,0,1:T(8,128)S(1)} fusion(f32[1536,4,112]{0,2,1:T(8,128)} %get-tuple-element.1145, f32[1536,4,273]{0,2,1:T(8,128)} %get-tuple-element.1144, f32[1536]{0:T(1024)S(1)} %compare_convert_fusion.4), kind=kOutput, calls=%fused_computation.6.clone.1 | convolution fusion | flops 2256107008 | bytes 9957120 | tf_op jit(solution)/shard_map/while/body/thf,thj->fhj/dot_general | solution.py:137
  206.0 12.9 %fusion.27 = f32[32,273,448]{2,0,1:T(8,128)} fusion(f32[5,273,448]{2,1,0:T(8,128)} %get-tuple-element.536, s32[5]{0:T(128)S(1)} %get-tuple-element.650, pred[5]{0:T(512)(128)(4,1)S(1)} %get-tuple-element.746), kind=kOutput, calls=%fused_computation.49 | convolution fusion | flops 234824000 | bytes 18101016 | tf_op jit(solution)/shard_map/ok,kfc->ofc/dot_general | solution.py:211
  225.7 49.4 %all-reduce = f32[32]{0:T(128)S(1)} all-reduce(f32[32]{0:T(128)S(1)} %dynamic-update-slice), channel_id=1, replica_groups=mesh['seq'=32,'tp'=4] {'seq'}, use_global_device_ids=true, to_apply=%add | all-reduce | flops 32 | bytes 256
  275.2 29.3 %all_gather.37 = f32[32,273,4]{1,2,0:T(4,128)} all-gather(f32[1,273,4]{1,2,0:T(4,128)S(1)} %copy-done.7), channel_id=1, replica_groups=mesh['seq'=32,'tp'=4] {'seq'}, dimensions={0}, use_global_device_ids=true | all-gather | bytes 144144 | tf_op jit(solution)/shard_map/all_gather | solution.py:156
  305.2 30.2 %while.83 = (s32[]{:T(128)}, f32[3,512,4,112]{1,3,2,0:T(8,128)}, f32[3,512,4]{1,2,0:T(4,128)S(1)}, s32[3]{0:T(128)S(1)}, s32[1536]{0:T(1024)S(1)}, /*index=5*/s3...) while((s32[]{:T(128)}, f32[3,512,4,112]{1,3,2,0:T(8,128)}, ...), condition=%wide.region_18.19_spmd.clone, body=%wide.region_13.18_spmd.clone.sunk | while | flops 278888544 | bytes 10109824 | solution.py:127
  318.3 5.1 while.85
  329.2 5.1 while.85
  342.7 27.1 %all_gather.35 = f32[32,273,4]{1,2,0:T(4,128)S(1)} all-gather(f32[1,273,4]{1,2,0:T(4,128)S(1)} %constant_dynamic-slice_fusion.3), channel_id=1, replica_groups=mesh['seq'=32,'tp'=4] {'seq'}, dimensions={0}, use_global_device_ids=true | all-gather | bytes 144144 | tf_op jit(solution)/shard_map/all_gather | solution.py:17
  369.8 30.5 %all-reduce.6.cloned.1.call-done = (f32[32,273,448]{2,0,1:T(8,128)}, f32[32,273,4]{1,2,0:T(4,128)}) async-done(((f32[32,273,448]{2,0,1:T(8,128)}, f32[32,273,4]{1,2,0:T(4,128)}), (f32[32,273,448]{2,0,1:T(8,128)}, f32[32,273,4]{1,2,0:T(4,128)})) %all-reduce.6.cloned.1.call-update) | async-done | bytes 15794704
  406.3 73.8 %all-gather.11.cloned.1.call-done = f32[32,273,448]{2,1,0:T(8,128)} async-done(((f32[1,273,448]{2,1,0:T(8,128)}), f32[32,273,448]{2,1,0:T(8,128)}) %all-gather.11.cloned.1.call-update) | async-done | bytes 15654928 | tf_op jit(solution)/shard_map/all_gather | solution.py:17
  480.1 107.6 %while.84 = (s32[]{:T(128)}, f32[273,448]{1,0:T(8,128)S(1)}, f32[273,4]{0,1:T(4,128)S(1)}, s32[]{:T(128)}, f32[32,273,448]{2,1,0:T(8,128)}, /*index=5*/f32[32,1]...) while((s32[]{:T(128)}, f32[273,448]{1,0:T(8,128)S(1)}, f32[273,4]{0,1:T(4,128)S(1)}, ...), condition=%wide.region_10.11_spmd.clone, body=%wide.region_9.10_spmd.clone.sunk | while | flops 493589 | bytes 1480903 | solution.py:26
  588.0 18.0 %multiply_add_fusion = f32[5,273,448]{2,0,1:T(8,128)} fusion(f32[273,448]{1,0:T(8,128)S(1)} %get-tuple-element.538, f32[5]{0:T(128)S(1)} %compare_select_fusion.2, f32[32,273,448]{2,1,0:T(8,128)} %all-gather.5.cloned.1.call-done, s32[5]{0:T(128)S(1)} %get-tuple-element.650, pred[5]{0:T(512)(128)(4,1)S(1)} %broadcast_compare_fusion, ...), kind=kOutput, calls=%fused_computation.51 | convolution fusion | flops 236047200 | bytes 18590258 | tf_op jit(solution)/shard_map/kr,rfc->kfc/dot_general | solution.py:163
  607.9 100.1 %while.81 = (s32[]{:T(128)}, f32[1536,4,112]{0,2,1:T(8,128)}, f32[1536,4]{0,1:T(4,128)S(1)}, s32[]{:T(128)}, s32[]{:T(128)}, /*index=5*/s32[1536]{0:T(1024)S(1)}...) while((s32[]{:T(128)}, f32[1536,4,112]{0,2,1:T(8,128)}, ...), condition=%wide.region_12.13_spmd, body=%wide.region_11.12_spmd.sunk | while | flops 2275826688 | bytes 42158388 | solution.py:204
  608.8 4.7 dynamic-slice_reduce_fusion.2
  615.1 9.3 %fusion.97 = f32[1536,4,112]{0,2,1:T(8,128)} fusion(f32[1536,4,112]{0,2,1:T(8,128)} %get-tuple-element.1189, f32[1536,4,273]{0,2,1:T(8,128)} %get-tuple-element.1207, f32[1536]{0:T(1024)S(1)} %compare_convert_fusion.5, f32[273,4,112]{2,1,0:T(4,128)S(1)} %reshape.238), kind=kOutput, calls=%fused_computation.33.clone.1 | convolution fusion | flops 2255683584 | bytes 12709632 | tf_op jit(solution)/shard_map/while/body/thf,fhj->thj/dot_general | solution.py:193
  628.8 4.7 dynamic-slice_reduce_fusion.2
  635.1 9.3 %fusion.97 = f32[1536,4,112]{0,2,1:T(8,128)} fusion(f32[1536,4,112]{0,2,1:T(8,128)} %get-tuple-element.1189, f32[1536,4,273]{0,2,1:T(8,128)} %get-tuple-element.1207, f32[1536]{0:T(1024)S(1)} %compare_convert_fusion.5, f32[273,4,112]{2,1,0:T(4,128)S(1)} %reshape.238), kind=kOutput, calls=%fused_computation.33.clone.1 | convolution fusion | flops 2255683584 | bytes 12709632 | tf_op jit(solution)/shard_map/while/body/thf,fhj->thj/dot_general | solution.py:193
  648.7 4.7 dynamic-slice_reduce_fusion.2
  655.1 9.3 %fusion.97 = f32[1536,4,112]{0,2,1:T(8,128)} fusion(f32[1536,4,112]{0,2,1:T(8,128)} %get-tuple-element.1189, f32[1536,4,273]{0,2,1:T(8,128)} %get-tuple-element.1207, f32[1536]{0:T(1024)S(1)} %compare_convert_fusion.5, f32[273,4,112]{2,1,0:T(4,128)S(1)} %reshape.238), kind=kOutput, calls=%fused_computation.33.clone.1 | convolution fusion | flops 2255683584 | bytes 12709632 | tf_op jit(solution)/shard_map/while/body/thf,fhj->thj/dot_general | solution.py:193
  675.0 9.3 %fusion.97 = f32[1536,4,112]{0,2,1:T(8,128)} fusion(f32[1536,4,112]{0,2,1:T(8,128)} %get-tuple-element.1189, f32[1536,4,273]{0,2,1:T(8,128)} %get-tuple-element.1207, f32[1536]{0:T(1024)S(1)} %compare_convert_fusion.5, f32[273,4,112]{2,1,0:T(4,128)S(1)} %reshape.238), kind=kOutput, calls=%fused_computation.33.clone.1 | convolution fusion | flops 2255683584 | bytes 12709632 | tf_op jit(solution)/shard_map/while/body/thf,fhj->thj/dot_general | solution.py:193
  695.0 9.3 %fusion.97 = f32[1536,4,112]{0,2,1:T(8,128)} fusion(f32[1536,4,112]{0,2,1:T(8,128)} %get-tuple-element.1189, f32[1536,4,273]{0,2,1:T(8,128)} %get-tuple-element.1207, f32[1536]{0:T(1024)S(1)} %compare_convert_fusion.5, f32[273,4,112]{2,1,0:T(4,128)S(1)} %reshape.238), kind=kOutput, calls=%fused_computation.33.clone.1 | convolution fusion | flops 2255683584 | bytes 12709632 | tf_op jit(solution)/shard_map/while/body/thf,fhj->thj/dot_general | solution.py:193
  (323 shorter events, 247.7 us)
Async XLA Ops:
  7.2 64.2 %all-gather.7.cloned.1.call-start = ((), (), s32[]{:S(2)}) async-start(), calls=%async_computation.1 | async-start | bytes 6881280 | tf_op jit(solution)/shard_map/all_gather | solution.py:47
  7.9 109.6 %all-gather.9.cloned.1.call-start = ((), (), s32[]{:S(2)}) async-start(), calls=%async_computation.2 | async-start | bytes 1892352 | tf_op jit(solution)/shard_map/all_gather | solution.py:61
  8.6 391.6 %all-reduce.6.cloned.1.call-start = ((), (), s32[]{:S(2)}) async-start(), calls=%async_computation.4 | async-start | bytes 36175872
  71.4 4.2 copy-start
  117.5 7.9 %copy-start.1 = (f32[1536,4,16,16]{0,3,2,1:T(8,128)S(1)}, f32[1536,4,16,16]{0,3,2,1:T(8,128)}, u32[]{:S(2)}) copy-start(f32[1536,4,16,16]{0,3,2,1:T(8,128)} %multiply_multiply_fusion) | copy-start | bytes 18874372
  117.5 7.9 %copy-start.2 = (f32[1536,4,16,16]{0,3,2,1:T(8,128)S(1)}, f32[1536,4,16,16]{0,3,2,1:T(8,128)}, u32[]{:S(2)}) copy-start(f32[1536,4,16,16]{0,3,2,1:T(8,128)} %multiply_multiply_fusion.1) | copy-start | bytes 18874372
  220.1 2.1 copy-start.4
  220.1 3.1 copy-start.9
  220.1 3.1 copy-start.10
  220.1 4.4 copy-start.8
  220.1 55.1 %copy-start.7 = (f32[1,273,4]{1,2,0:T(4,128)S(1)}, f32[1,273,4]{1,2,0:T(4,128)}, u32[]{:S(2)}) copy-start(f32[1,273,4]{1,2,0:T(4,128)} %param.27) | copy-start | bytes 13108
  220.1 260.0 %all-gather.11.cloned.1.call-start = ((), (), s32[]{:S(2)}) async-start(), calls=%async_computation.3 | async-start | bytes 18923520 | tf_op jit(solution)/shard_map/all_gather | solution.py:17
  222.2 365.8 %all-gather.5.cloned.1.call-start = ((), (), s32[]{:S(2)}) async-start(), calls=%async_computation | async-start | bytes 18923520 | tf_op jit(solution)/shard_map/all_gather | solution.py:155
  339.1 63.0 %copy-start.5 = (f32[1,273,448]{2,0,1:T(1,128)S(1)}, f32[1,273,448]{2,0,1:T(1,128)}, u32[]{:S(2)}) copy-start(f32[1,273,448]{2,0,1:T(1,128)} %param.26) | copy-start | bytes 1467652
  480.1 107.6 %copy-start.6 = (f32[32,273,4]{1,2,0:T(4,128)S(1)}, f32[32,273,4]{1,2,0:T(4,128)}, u32[]{:S(2)}) copy-start(f32[32,273,4]{1,2,0:T(4,128)} %all_gather.37) | copy-start | bytes 419332
  613.5 10.9 %slice-start = ((s8[6881280]{0:T(1024)(128)(4,1)}), s8[2686976]{0:T(1024)(128)(4,1)S(1)}, s32[]{:S(2)}) async-start(s8[6881280]{0:T(1024)(128)(4,1)} %bitcast.130), calls=%async_computation.5 | async-start | bytes 5373952 | tf_op jit(solution)/shard_map/while
  615.1 9.3 %slice-start.1 = ((s8[6881280]{0:T(1024)(128)(4,1)}), s8[4194304]{0:T(1024)(128)(4,1)S(1)}, s32[]{:S(2)}) async-start(s8[6881280]{0:T(1024)(128)(4,1)} %bitcast.130), calls=%async_computation.6 | async-start | bytes 8388608 | tf_op jit(solution)/shard_map/while
  633.5 10.9 %slice-start = ((s8[6881280]{0:T(1024)(128)(4,1)}), s8[2686976]{0:T(1024)(128)(4,1)S(1)}, s32[]{:S(2)}) async-start(s8[6881280]{0:T(1024)(128)(4,1)} %bitcast.130), calls=%async_computation.5 | async-start | bytes 5373952 | tf_op jit(solution)/shard_map/while
  635.1 9.4 %slice-start.1 = ((s8[6881280]{0:T(1024)(128)(4,1)}), s8[4194304]{0:T(1024)(128)(4,1)S(1)}, s32[]{:S(2)}) async-start(s8[6881280]{0:T(1024)(128)(4,1)} %bitcast.130), calls=%async_computation.6 | async-start | bytes 8388608 | tf_op jit(solution)/shard_map/while
  653.5 10.9 %slice-start = ((s8[6881280]{0:T(1024)(128)(4,1)}), s8[2686976]{0:T(1024)(128)(4,1)S(1)}, s32[]{:S(2)}) async-start(s8[6881280]{0:T(1024)(128)(4,1)} %bitcast.130), calls=%async_computation.5 | async-start | bytes 5373952 | tf_op jit(solution)/shard_map/while
  655.0 9.4 %slice-start.1 = ((s8[6881280]{0:T(1024)(128)(4,1)}), s8[4194304]{0:T(1024)(128)(4,1)S(1)}, s32[]{:S(2)}) async-start(s8[6881280]{0:T(1024)(128)(4,1)} %bitcast.130), calls=%async_computation.6 | async-start | bytes 8388608 | tf_op jit(solution)/shard_map/while
  673.4 10.9 %slice-start = ((s8[6881280]{0:T(1024)(128)(4,1)}), s8[2686976]{0:T(1024)(128)(4,1)S(1)}, s32[]{:S(2)}) async-start(s8[6881280]{0:T(1024)(128)(4,1)} %bitcast.130), calls=%async_computation.5 | async-start | bytes 5373952 | tf_op jit(solution)/shard_map/while
  675.0 9.4 %slice-start.1 = ((s8[6881280]{0:T(1024)(128)(4,1)}), s8[4194304]{0:T(1024)(128)(4,1)S(1)}, s32[]{:S(2)}) async-start(s8[6881280]{0:T(1024)(128)(4,1)} %bitcast.130), calls=%async_computation.6 | async-start | bytes 8388608 | tf_op jit(solution)/shard_map/while
  693.4 10.9 %slice-start = ((s8[6881280]{0:T(1024)(128)(4,1)}), s8[2686976]{0:T(1024)(128)(4,1)S(1)}, s32[]{:S(2)}) async-start(s8[6881280]{0:T(1024)(128)(4,1)} %bitcast.130), calls=%async_computation.5 | async-start | bytes 5373952 | tf_op jit(solution)/shard_map/while
  695.0 9.4 %slice-start.1 = ((s8[6881280]{0:T(1024)(128)(4,1)}), s8[4194304]{0:T(1024)(128)(4,1)S(1)}, s32[]{:S(2)}) async-start(s8[6881280]{0:T(1024)(128)(4,1)} %bitcast.130), calls=%async_computation.6 | async-start | bytes 8388608 | tf_op jit(solution)/shard_map/while
  708.0 3.6 copy-start.3
Sparse Core Ops, SparseCore 0:
  9.7 61.6 all-gather.6
  73.6 43.7 all-gather.8
  220.2 179.9 all-reduce.5
  402.9 77.1 all-gather.10
  482.2 75.7 all-gather.4
where the time goes:
time: 735 us; the launch traced here: 724 us
  other arithmetic  164 us (22%)
  matrix products  162 us (22%)
  blocking collectives  154 us (21%)
  waiting for transfers between devices  147 us (20%)
  local copies, waits for them, and re-layouts  66.5 us (9%)
  between operations  16.9 us (2%)
  loops' own time  15 us (2%)
    select_n x62, other arithmetic, hop(): jnp.where(position < mine, new, old)  88.8 us
    all_gather x1, waiting for transfers between devices, carried_in(): pieces = jax.tree.map(lambda part: lax.all_gather(part, axis), value)  73.8 us
    unnamed x1, blocking collectives  49.4 us
    dot_general x5, matrix products, prior_terms(): jnp.einsum('thf,fhj->thj', phi_q, slot_state, precision=full_precision)  46.5 us
    dot_general x5, matrix products, slot_terms(): jnp.einsum('thf,thj->fhj', weighted, value_f, precision=full_precision)  44.2 us
    all_gather x1, waiting for transfers between devices, local(): lax.all_gather(w_value, 'seq', axis=0, tiled=True)  33.6 us
    unnamed x6, waiting for transfers between devices  31.9 us
    all_gather x1, blocking collectives, local(): piece_norm = lax.all_gather(init_norm, 'seq', axis=0, tiled=True)  29.3 us
  transfers between devices with their start and end apart: 5, of which 4 were waited for; matrix products, arithmetic and copies ran while one was open for 23% of the time, Pallas kernels for 0%

commit v1 on v0

v1 whole, which is shorter than its diff:
```python
import functools
import math

import jax
import jax.numpy as jnp
import numpy as np
from jax import lax
from jax.experimental import pallas as pl
from jax.experimental.pallas import tpu as pltpu
from jax.sharding import PartitionSpec as P

FD = 16
HD = 4
HV = 112
FEAT = 273
ENDS = 4
SLOTS = 5
ROWS = 192
MESH = pl.DeviceIdType.MESH
F32 = jnp.float32
BF16 = jnp.bfloat16


def tables(norm):
    e1 = np.zeros((FD, 256), np.float32)
    e2 = np.zeros((FD, 256), np.float32)
    b1 = np.zeros((256,), np.float32)
    b2 = np.zeros((256,), np.float32)
    coef = np.zeros((256,), np.float32)
    fold = np.zeros((ROWS, FEAT), np.float32)
    fold_scale = np.zeros((ROWS, 1), np.float32)
    spread = np.zeros((FEAT, ROWS), np.float32)
    spread_scale = np.zeros((FEAT, 1), np.float32)
    root = math.sqrt(2.0 * FD)
    for d in range(9):
        for i in range(FD if d < 8 else 8):
            f = d * FD + i
            j = (i + d) % FD
            e1[i, f] = 1.0
            e2[j, f] = 1.0
            coef[f] = 1.0 / 32.0 if d == 0 else 1.0 / 16.0
            for a, b in {(i, j), (j, i)}:
                g = 1 + FD + a * FD + b
                fold[f, g] = 1.0
                spread[g, f] = 1.0
                spread_scale[g, 0] = 1.0 / (coef[f] * root * norm)
            fold_scale[f, 0] = norm / root
    b1[136] = 1.0
    coef[136] = 1.0
    fold[136, 0] = 1.0
    fold_scale[136, 0] = norm
    spread[0, 136] = 1.0
    spread_scale[0, 0] = 1.0 / norm
    for i in range(FD):
        f = 144 + i
        e1[i, f] = 1.0
        b2[f] = 1.0
        coef[f] = 0.25
        fold[f, 1 + i] = 1.0
        fold_scale[f, 0] = norm / 2.0
        spread[1 + i, f] = 1.0
        spread_scale[1 + i, 0] = 2.0 / norm
    q1 = np.zeros((128, HD * 256), np.float32)
    q2 = np.zeros((128, HD * 256), np.float32)
    k1 = np.zeros((HD * 256, 128), np.float32)
    k2 = np.zeros((HD * 256, 128), np.float32)
    for h in range(HD):
        cols = slice(256 * h, 256 * h + 256)
        q1[16 * h : 16 * h + 16, cols] = e1
        q2[16 * h : 16 * h + 16, cols] = e2
        k1[cols, 64 + 16 * h : 80 + 16 * h] = (e1 * coef).T
        k2[cols, 64 + 16 * h : 80 + 16 * h] = e2.T
    bq = np.stack([np.tile(b1, HD), np.tile(b2, HD)])
    bk = np.stack([np.tile(b1 * coef, HD), np.tile(b2, HD)], axis=1)
    pack = np.zeros((HD * 128, HD * HV), np.float32)
    pack_n = np.zeros((HD * 128, 128), np.float32)
    for h in range(HD):
        for j in range(HV):
            pack[128 * h + j, HV * h + j] = 1.0
        pack_n[128 * h + HV, h] = 1.0
    bf = lambda x: jnp.asarray(x, BF16)
    f32 = lambda x: jnp.asarray(x, F32)
    return (
        bf(q1), bf(q2), bf(k1), bf(k2), f32(bq), f32(bk), bf(fold), f32(fold_scale), bf(spread),
        f32(spread_scale), bf(pack), bf(pack.T), bf(pack_n), bf(pack_n.T[:HD]),
    )


def dot(a, b):
    return jnp.dot(a, b, preferred_element_type=F32)


def kernel(
    S, Z, C,
    lengths, owner, resume, tokens, wq, wk, wv, init, norm,
    q1, q2, k1, k2, bq, bk, fold, fold_s, spread, spread_s, pack, unpack, pack_n, unpack_n,
    out, fstate, fnorm,
    gat, wsend, wrecv, wall, stage, isend, irecv, ssend, srecv, start, lsend, lrecv, csend, crecv,
    psiq, num, eacc, run, ftab,
    ends, first, inv,
    own_sem, dsend, drecv, fsend, frecv, xsend, xrecv,
):
    T = out.shape[0]
    NC = T // C
    H = C // 2
    SR = HD * ROWS // S
    PH = S // HD
    WR = wq.shape[0]
    FW = tokens.shape[1]
    me = lax.axis_index("seq")
    mz = lax.axis_index("tp")
    up, down = lax.rem(mz + 1, Z), lax.rem(mz + Z - 1, Z)

    barrier = pltpu.get_barrier_semaphore()

    def greet(i, x):
        pl.semaphore_signal(
            barrier, inc=1, device_id={"seq": lax.rem(me + i, S)}, device_id_type=MESH
        )
        return x

    lax.fori_loop(1, S, greet, 0)
    for z in (up, down):
        pl.semaphore_signal(barrier, inc=1, device_id={"tp": z}, device_id_type=MESH)

    own = pltpu.make_async_copy(tokens, gat.at[mz], own_sem)
    own.start()
    wsend[:, :64] = wq[...]
    wsend[:, 64:128] = wk[...]
    wsend[:, 128:] = dot(wv[...], unpack[...]).astype(BF16)
    full = init[0]
    hi = full.astype(BF16)
    lo = (full - hi.astype(F32)).astype(BF16)
    folded = (dot(fold[...], hi) + dot(fold[...], lo)) * fold_s[...]
    full = norm[0]
    hi = full.astype(BF16)
    lo = (full - hi.astype(F32)).astype(BF16)
    folded_n = (dot(fold[...], hi) + dot(fold[...], lo)) * fold_s[...]
    stage[...] = dot(folded.astype(BF16), unpack[...]) + dot(folded_n.astype(BF16), unpack_n[...])
    for s in range(S):
        h, k = s // PH, s % PH
        isend[s] = stage[SR * k : SR * k + SR, 128 * h : 128 * h + 128].astype(BF16)
    pl.semaphore_wait(barrier, S + 1)

    def direct(way, c):
        rows = pl.ds(c * C, C)
        return pltpu.make_async_remote_copy(
            src_ref=tokens.at[rows],
            dst_ref=gat.at[mz, rows],
            send_sem=dsend.at[way, c],
            recv_sem=drecv.at[way, c],
            device_id={"tp": up if way == 0 else down},
            device_id_type=MESH,
        )

    def onward(way, c):
        rows = pl.ds(c * C + way * H, H)
        place = gat.at[down if way == 0 else up, rows]
        return pltpu.make_async_remote_copy(
            src_ref=place,
            dst_ref=place,
            send_sem=fsend.at[way, c],
            recv_sem=frecv.at[way, c],
            device_id={"tp": up if way == 0 else down},
            device_id_type=MESH,
        )

    def exchange(src, dst, n):
        keep = pltpu.make_async_copy(src(me), dst(me), xrecv.at[n])
        keep.start()

        def send(i, x):
            peer = lax.rem(me + i, S)
            pltpu.make_async_remote_copy(
                src_ref=src(peer),
                dst_ref=dst(me),
                send_sem=xsend.at[n],
                recv_sem=xrecv.at[n],
                device_id={"seq": peer},
                device_id_type=MESH,
            ).start()
            return x

        lax.fori_loop(1, S, send, 0)

    def arrived(dst, n):
        pltpu.make_async_copy(dst, dst, xrecv.at[n]).wait()

    def sent(buf, n):
        part = buf.at[pl.ds(0, S - 1)]
        pltpu.make_async_copy(part, part, xsend.at[n]).wait()

    for c in range(3):
        for way in (0, 1):
            direct(way, c).start()
    exchange(lambda p: isend.at[p], lambda p: irecv.at[p], 0)
    exchange(lambda p: wsend, lambda p: wrecv.at[p], 1)

    total = jnp.int32(0)
    for r in range(S):
        total = total + lengths[r]
        ends[r] = total

    def count(b, x):
        before = jnp.int32(0)
        back = jnp.int32(0)
        for r in range(S):
            before = before + (ends[r] <= b * T).astype(jnp.int32)
            back = back + jnp.where(owner[r] == b, r, 0)
        first[b] = before
        inv[b] = jnp.minimum(back, S - 1)
        return x

    lax.fori_loop(0, S, count, 0)
    first[S] = jnp.int32(S)

    arrived(irecv, 0)

    def pick(b, x):
        for j in range(SLOTS):
            r = first[b] + j
            safe = jnp.minimum(r, S - 1)
            weight = jnp.where(r < S, resume[safe], 0).astype(F32)
            ssend[b, j] = (irecv[owner[safe]].astype(F32) * weight).astype(BF16)
        return x

    lax.fori_loop(0, S, pick, 0)
    exchange(lambda p: ssend.at[p], lambda p: srecv.at[p], 2)

    def relay(c):
        for way in (0, 1):
            direct(way, c).wait_recv()
            onward(way, c).start()
        if c + 3 < NC:
            for way in (0, 1):
                direct(way, c + 3).start()

    base = me * T
    req = first[me]
    stops = []
    for j in range(ENDS):
        r = req + j
        stop = ends[jnp.minimum(r, S - 1)] - base
        stops.append(jnp.where(r < S, stop, 4 * T))

    def slot_of(pos):
        slot = jnp.zeros_like(pos)
        for stop in stops:
            slot = slot + jnp.where(pos >= stop, 1, 0)
        return slot

    for c in range(4):
        relay(c)

    run[...] = jnp.zeros_like(run)
    eacc[...] = jnp.zeros_like(eacc)
    arrived(wrecv, 1)
    for s in range(S):
        wall[WR * s : WR * s + WR, :] = wrecv[s].astype(wall.dtype)
    own.wait()

    lane64 = lax.broadcasted_iota(jnp.int32, (1, 64), 1)
    lane512 = lax.broadcasted_iota(jnp.int32, (1, HD * 128), 1)
    ones_col = lax.rem(lane512, 128) == HV

    def chunk(c, x):
        @pl.when(c == 2)
        def _():
            relay(4)

        @pl.when(c == 4)
        def _():
            relay(5)

        for way in (0, 1):
            onward(way, c).wait_recv()
        rows = pl.ds(pl.multiple_of(c * C, C), C)
        acc = jnp.zeros((C, 640), F32)
        for z in range(Z):
            acc = acc + dot(gat[z, rows, :], wall[z * FW : (z + 1) * FW, :].astype(BF16))
        qk32 = acc[:, :128]
        qk = qk32.astype(BF16)
        v = jnp.where(ones_col, 1.0, acc[:, 128:].astype(BF16).astype(F32))
        qkT = jnp.transpose(qk.astype(F32)).astype(BF16)
        pq = (dot(qk, q1[...]) * (dot(qk, q2[...]) + bq[1:2, :]) + bq[0:1, :]).astype(BF16)
        psiq[rows, :] = pq
        pk = (dot(k1[...], qkT) * (dot(k2[...], qkT) + bk[:, 1:2]) + bk[:, 0:1]).astype(BF16)
        pos_col = c * C + lax.broadcasted_iota(jnp.int32, (C, 1), 0)
        pos_row = c * C + lax.broadcasted_iota(jnp.int32, (1, C), 1)
        slot_col = slot_of(pos_col)
        slot_row = slot_of(pos_row)
        slot_top = jnp.int32(0)
        slot_next = jnp.int32(0)
        for stop in stops:
            slot_top = slot_top + (c * C >= stop).astype(jnp.int32)
            slot_next = slot_next + (c * C + C >= stop).astype(jnp.int32)
        allowed = (slot_col == slot_row) & (pos_row <= pos_col)
        from_top = (slot_col == slot_top).astype(F32)
        keep = (slot_top == slot_next).astype(F32)
        q64 = qk32[:, :64].astype(BF16).astype(F32)
        for h in range(HD):
            head = (lane64 >= 16 * h) & (lane64 < 16 * h + 16)
            a = dot(jnp.where(head, q64, 0.0).astype(BF16), qkT[64:, :]) * 0.25
            weight = jnp.where(allowed, 1.0 + a + 0.5 * a * a, 0.0).astype(BF16)
            vh = v[:, 128 * h : 128 * h + 128]
            state = run[h]
            s_hi = state.astype(BF16)
            s_lo = (state - s_hi.astype(F32)).astype(BF16)
            pqh = pq[:, 256 * h : 256 * h + 256]
            both = dot(pqh, jnp.concatenate([s_hi, s_lo], axis=1))
            num[rows, 128 * h : 128 * h + 128] = dot(weight, vh.astype(BF16)) + from_top * (
                both[:, :128] + both[:, 128:]
            )
            parts = []
            for j in range(ENDS):
                mark = (slot_col == j) & (stops[j] <= T)
                parts.append(jnp.where(mark, vh, 0.0).astype(BF16))
            parts.append(jnp.where(slot_col == slot_next, vh, 0.0).astype(BF16))
            made = dot(pk[256 * h : 256 * h + 256, :], jnp.concatenate(parts, axis=1))
            eacc[h] += made[:ROWS, : ENDS * 128]
            run[h] = keep * state + made[:, ENDS * 128 :]
        return x

    lax.fori_loop(0, NC, chunk, 0)

    for s in range(S):
        h, k = s // PH, s % PH
        rows = slice(SR * k, SR * k + SR)
        lsend[s, ENDS] = run[h, rows, :].astype(BF16)
        for j in range(ENDS):
            lsend[s, j] = eacc[h, rows, 128 * j : 128 * j + 128].astype(BF16)
    exchange(lambda p: lsend.at[p], lambda p: lrecv.at[p], 3)

    arrived(srecv, 2)
    for s in range(S):
        h, k = s // PH, s % PH
        for j in range(SLOTS):
            start[h, SR * k : SR * k + SR, 128 * j : 128 * j + 128] = srecv[s, j].astype(F32)
    start[:, ROWS:, :] = jnp.zeros((HD, 256 - ROWS, SLOTS * 128), F32)

    def begin(c, x):
        rows = pl.ds(pl.multiple_of(c * C, C), C)
        slot_col = slot_of(c * C + lax.broadcasted_iota(jnp.int32, (C, 1), 0))
        for h in range(HD):
            got = dot(psiq[rows, 256 * h : 256 * h + 256], start[h].astype(BF16))
            add = jnp.zeros((C, 128), F32)
            for j in range(SLOTS):
                add = jnp.where(slot_col == j, got[:, 128 * j : 128 * j + 128], add)
            num[rows, 128 * h : 128 * h + 128] += add
        return x

    lax.fori_loop(0, NC, begin, 0)

    arrived(lrecv, 3)

    def carry(b, c):
        csend[b, 0] = c.astype(BF16)
        go_on = (first[b] == first[b + 1]).astype(F32)
        ftab[b] = c
        return c * go_on + lrecv[b, ENDS].astype(F32)

    lax.fori_loop(0, S, carry, jnp.zeros((SR, 128), F32))

    def finish(o, x):
        r = inv[o]
        b = jnp.clip(lax.div(ends[r] - 1, T), 0, S - 1)
        j = jnp.clip(r - first[b], 0, ENDS - 1)
        lead = (j == 0).astype(F32)
        csend[o, 1] = (lrecv[b, j].astype(F32) + lead * ftab[b]).astype(BF16)
        return x

    lax.fori_loop(0, S, finish, 0)
    exchange(lambda p: csend.at[p], lambda p: crecv.at[p], 4)
    arrived(crecv, 4)
    for s in range(S):
        h, k = s // PH, s % PH
        rows = slice(SR * k, SR * k + SR)
        run[h, rows, :] = crecv[s, 0].astype(F32)
        stage[rows, 128 * h : 128 * h + 128] = crecv[s, 1].astype(F32)
    run[:, ROWS:, :] = jnp.zeros((HD, 256 - ROWS, 128), F32)

    def close(c, x):
        rows = pl.ds(pl.multiple_of(c * C, C), C)
        slot_col = slot_of(c * C + lax.broadcasted_iota(jnp.int32, (C, 1), 0))
        parts = []
        for h in range(HD):
            got = dot(psiq[rows, 256 * h : 256 * h + 256], run[h].astype(BF16))
            both = num[rows, 128 * h : 128 * h + 128] + jnp.where(slot_col == 0, got, 0.0)
            parts.append((both / both[:, HV : HV + 1]).astype(BF16))
        out[rows, :] = dot(jnp.concatenate(parts, axis=1), pack[...]).astype(BF16)
        return x

    lax.fori_loop(0, NC, close, 0)

    got = stage[...].astype(BF16)
    flag = resume[inv[me]].astype(F32)
    fstate[0] = flag * init[0] + spread_s[...] * dot(spread[...], dot(got, pack[...]).astype(BF16))
    moved = spread_s[...] * dot(spread[...], dot(got, pack_n[...]).astype(BF16))
    fnorm[0] = flag * norm[0] + moved[:, :HD]

    for c in range(NC):
        for way in (0, 1):
            direct(way, c).wait_send()
            onward(way, c).wait_send()
    for n, buf in ((0, isend), (1, wrecv), (2, ssend), (3, lsend), (4, csend)):
        sent(buf, n)


def local(tokens, wq, wk, wv, lengths, owner, resume, init, norm):
    S, Z = lax.axis_size("seq"), lax.axis_size("tp")
    T, FW = tokens.shape
    C = T // 6
    SR = HD * ROWS // S
    consts = tables(float(T * S // 2))
    smem = pl.BlockSpec(memory_space=pltpu.SMEM)
    vmem = pl.BlockSpec(memory_space=pltpu.VMEM)
    hbm = pl.BlockSpec(memory_space=pl.ANY)
    return pl.pallas_call(
        functools.partial(kernel, S, Z, C),
        out_shape=(
            jax.ShapeDtypeStruct((T, HD * HV), BF16),
            jax.ShapeDtypeStruct(init.shape, F32),
            jax.ShapeDtypeStruct(norm.shape, F32),
        ),
        in_specs=[smem] * 3 + [hbm] + [vmem] * (5 + len(consts)),
        out_specs=(vmem, vmem, vmem),
        scratch_shapes=[
            pltpu.VMEM((Z, T, FW), BF16),
            pltpu.VMEM((wq.shape[0], 640), BF16),
            pltpu.VMEM((S, wq.shape[0], 640), BF16),
            pltpu.VMEM((S * wq.shape[0], 640), F32),
            pltpu.VMEM((ROWS, HD * 128), F32),
            pltpu.VMEM((S, SR, 128), BF16),
            pltpu.VMEM((S, SR, 128), BF16),
            pltpu.VMEM((S, SLOTS, SR, 128), BF16),
            pltpu.VMEM((S, SLOTS, SR, 128), BF16),
            pltpu.VMEM((HD, 256, SLOTS * 128), F32),
            pltpu.VMEM((S, SLOTS, SR, 128), BF16),
            pltpu.VMEM((S, SLOTS, SR, 128), BF16),
            pltpu.VMEM((S, 2, SR, 128), BF16),
            pltpu.VMEM((S, 2, SR, 128), BF16),
            pltpu.VMEM((T, HD * 256), BF16),
            pltpu.VMEM((T, HD * 128), F32),
            pltpu.VMEM((HD, ROWS, ENDS * 128), F32),
            pltpu.VMEM((HD, 256, 128), F32),
            pltpu.VMEM((S, SR, 128), F32),
            pltpu.SMEM((S,), jnp.int32),
            pltpu.SMEM((S + 1,), jnp.int32),
            pltpu.SMEM((S,), jnp.int32),
            pltpu.SemaphoreType.DMA,
            pltpu.SemaphoreType.DMA((2, 6)),
            pltpu.SemaphoreType.DMA((2, 6)),
            pltpu.SemaphoreType.DMA((2, 6)),
            pltpu.SemaphoreType.DMA((2, 6)),
            pltpu.SemaphoreType.DMA((5,)),
            pltpu.SemaphoreType.DMA((5,)),
        ],
        compiler_params=pltpu.CompilerParams(
            collective_id=0, has_side_effects=True, vmem_limit_bytes=60 * 2**20
        ),
    )(lengths, owner, resume, tokens, wq, wk, wv, init, norm, *consts)


def solution(mesh):
    in_specs = (
        P("seq", "tp"),
        P("seq", "tp"),
        P("seq", "tp"),
        P("seq", "tp"),
        P(),
        P(),
        P(),
        P("seq", None, "tp"),
        P("seq", None, "tp"),
    )
    out_specs = (P("seq", "tp"), P("seq", None, "tp"), P("seq", None, "tp"))
    return jax.shard_map(local, mesh=mesh, in_specs=in_specs, out_specs=out_specs, check_vma=False)
```

time: 735 us -> 115 us (0.16)
  the two profiles are of different devices: /device:TPU:7 before, /device:TPU:5 now
where the time goes in v1:
time: 115 us; the launch traced here: 114 us
  Pallas kernels  103 us (90%)
  local copies, waits for them, and re-layouts  10.6 us (9%)
    pallas_call x1, Pallas kernels, local(): pl.pallas_call(functools.partial(kernel, S, Z, C), out_shape=(jax.ShapeDt...  103 us
    unnamed x7, local copies, waits for them, and re-layouts  5.97 us
    pallas_call x3, local copies, waits for them, and re-layouts, local(): pl.pallas_call(functools.partial(kernel, S, Z, C), out_shape=(jax.ShapeDt...  4.66 us

profile of v1, /device:TPU:5, one launch (start us, length us, event | category | flops | bytes accessed | tf_op | source)
XLA Modules:
  0.0 114.4 jit_solution(12206050736441991288)
XLA Ops:
  0.6 1.5 %copy.28.norm = f32[1,273,4]{2,1,0:T(8,128)} copy(f32[1,273,4]{1,2,0:T(4,128)} %param.31) | data formatting | bytes 8736 | tf_op args[8]
  2.1 1.9 %copy.27.init = f32[1,273,448]{2,1,0:T(8,128)} copy(f32[1,273,448]{2,0,1:T(1,128)} %param.30) | data formatting | bytes 978432 | tf_op args[7]
  4.0 2.6 %copy.26.tokens = bf16[1536,448]{1,0:T(8,128)(2,1)} copy(bf16[1536,448]{0,1:T(8,128)(2,1)} %param.23) | data formatting | bytes 2752512 | tf_op args[0]
  6.6 103.1 %shard_map.238 = (bf16[1536,448]{1,0:T(8,128)(2,1)}, f32[1,273,448]{2,1,0:T(8,128)}, f32[1,273,4]{2,1,0:T(8,128)}) custom-call(s32[32]{0:T(128)} %lengths.1, s32[32]{0:T(128)} %owner.1, s32[32]{0:T(128)} %resume.1, bf16[1536,448]{1,0:T(8,128)(2,1)} %copy.26.tokens, bf16[56,64]{1,0:T(8,128)(2,1)} %wq.1, bf16[56,64]{1,0:T(8,128)(2,1)} %wk.1, ...), custom_call_target="tpu_custom_call" | custom-call | tf_op jit(solution)/shard_map/pallas_call | solution.py:418
  109.7 0.0 copy-start.1
  109.7 0.0 copy-start
  109.7 2.6 %copy.29 = bf16[1536,448]{0,1:T(8,128)(2,1)} copy(bf16[1536,448]{1,0:T(8,128)(2,1)} %get-tuple-element.3) | data formatting | bytes 2752512 | tf_op jit(solution)/shard_map/pallas_call | solution.py:418
  112.3 0.0 copy-done.1
  112.3 0.7 copy.31
  113.0 0.0 copy-done
  113.0 1.4 %copy.30 = f32[1,273,448]{2,0,1:T(1,128)} copy(f32[1,273,448]{2,1,0:T(8,128)S(1)} %copy-done) | data formatting | bytes 978432 | tf_op jit(solution)/shard_map/pallas_call | solution.py:418
Async XLA Ops:
  109.7 2.6 %copy-start.1 = (f32[1,273,4]{2,1,0:T(8,128)S(1)}, f32[1,273,4]{2,1,0:T(8,128)}, u32[]{:S(2)}) copy-start(f32[1,273,4]{2,1,0:T(8,128)} %get-tuple-element.5) | copy-start | bytes 13108
  109.7 3.3 %copy-start = (f32[1,273,448]{2,1,0:T(8,128)S(1)}, f32[1,273,448]{2,1,0:T(8,128)}, u32[]{:S(2)}) copy-start(f32[1,273,448]{2,1,0:T(8,128)} %get-tuple-element.4) | copy-start | bytes 1467652

commit v2 on v1

--- a/solution.py
+++ b/solution.py
@@ -82,31 +82,35 @@
     f32 = lambda x: jnp.asarray(x, F32)
     return (
         bf(q1), bf(q2), bf(k1), bf(k2), f32(bq), f32(bk), bf(fold), f32(fold_scale), bf(spread),
-        f32(spread_scale), bf(pack), bf(pack.T), bf(pack_n), bf(pack_n.T[:HD]),
+        f32(spread_scale), f32(spread_scale.T), bf(pack), bf(pack.T), bf(pack_n.T[:HD]),
     )
 
 
 def dot(a, b):
     return jnp.dot(a, b, preferred_element_type=F32)
+
+
+def dot_nt(a, b):
+    return lax.dot_general(a, b, (((1,), (1,)), ((), ())), preferred_element_type=F32)
 
 
 def kernel(
     S, Z, C,
     lengths, owner, resume, tokens, wq, wk, wv, init, norm,
-    q1, q2, k1, k2, bq, bk, fold, fold_s, spread, spread_s, pack, unpack, pack_n, unpack_n,
+    q1, q2, k1, k2, bq, bk, fold, fold_s, spread, spread_s, spread_t, pack, unpack, unpack_n,
     out, fstate, fnorm,
-    gat, wsend, wrecv, wall, stage, isend, irecv, ssend, srecv, start, lsend, lrecv, csend, crecv,
+    gat, wsend, wrecv, wall, wallt, stage, isend, irecv, ssend, srecv, start, lsend, lrecv, csend, crecv,
     psiq, num, eacc, run, ftab,
     ends, first, inv,
     own_sem, dsend, drecv, fsend, frecv, xsend, xrecv,
 ):
-    T = out.shape[0]
+    T = out.shape[1]
     NC = T // C
     H = C // 2
     SR = HD * ROWS // S
     PH = S // HD
     WR = wq.shape[0]
-    FW = tokens.shape[1]
+    FW = tokens.shape[0]
     me = lax.axis_index("seq")
     mz = lax.axis_index("tp")
     up, down = lax.rem(mz + 1, Z), lax.rem(mz + Z - 1, Z)
@@ -135,7 +139,7 @@
     full = norm[0]
     hi = full.astype(BF16)
     lo = (full - hi.astype(F32)).astype(BF16)
-    folded_n = (dot(fold[...], hi) + dot(fold[...], lo)) * fold_s[...]
+    folded_n = (dot_nt(fold[...], hi) + dot_nt(fold[...], lo)) * fold_s[...]
     stage[...] = dot(folded.astype(BF16), unpack[...]) + dot(folded_n.astype(BF16), unpack_n[...])
     for s in range(S):
         h, k = s // PH, s % PH
@@ -145,8 +149,8 @@
     def direct(way, c):
         rows = pl.ds(c * C, C)
         return pltpu.make_async_remote_copy(
-            src_ref=tokens.at[rows],
-            dst_ref=gat.at[mz, rows],
+            src_ref=tokens.at[:, rows],
+            dst_ref=gat.at[mz, :, rows],
             send_sem=dsend.at[way, c],
             recv_sem=drecv.at[way, c],
             device_id={"tp": up if way == 0 else down},
@@ -155,7 +159,7 @@
 
     def onward(way, c):
         rows = pl.ds(c * C + way * H, H)
-        place = gat.at[down if way == 0 else up, rows]
+        place = gat.at[down if way == 0 else up, :, rows]
         return pltpu.make_async_remote_copy(
             src_ref=place,
             dst_ref=place,
@@ -257,11 +261,12 @@
     arrived(wrecv, 1)
     for s in range(S):
         wall[WR * s : WR * s + WR, :] = wrecv[s].astype(wall.dtype)
+    for z in range(Z):
+        wallt[z] = jnp.transpose(wall[z * FW : (z + 1) * FW, :]).astype(BF16)
     own.wait()
 
     lane64 = lax.broadcasted_iota(jnp.int32, (1, 64), 1)
-    lane512 = lax.broadcasted_iota(jnp.int32, (1, HD * 128), 1)
-    ones_col = lax.rem(lane512, 128) == HV
+    ones_row = lax.broadcasted_iota(jnp.int32, (128, 1), 0) == HV
 
     def chunk(c, x):
         @pl.when(c == 2)
@@ -275,13 +280,12 @@
         for way in (0, 1):
             onward(way, c).wait_recv()
         rows = pl.ds(pl.multiple_of(c * C, C), C)
-        acc = jnp.zeros((C, 640), F32)
+        acc = jnp.zeros((640, C), F32)
         for z in range(Z):
-            acc = acc + dot(gat[z, rows, :], wall[z * FW : (z + 1) * FW, :].astype(BF16))
-        qk32 = acc[:, :128]
+            acc = acc + dot(wallt[z], gat[z, :, rows])
+        qkT = acc[:128].astype(BF16)
+        qk32 = jnp.transpose(acc[:128])
         qk = qk32.astype(BF16)
-        v = jnp.where(ones_col, 1.0, acc[:, 128:].astype(BF16).astype(F32))
-        qkT = jnp.transpose(qk.astype(F32)).astype(BF16)
         pq = (dot(qk, q1[...]) * (dot(qk, q2[...]) + bq[1:2, :]) + bq[0:1, :]).astype(BF16)
         psiq[rows, :] = pq
         pk = (dot(k1[...], qkT) * (dot(k2[...], qkT) + bk[:, 1:2]) + bk[:, 0:1]).astype(BF16)
@@ -302,21 +306,21 @@
             head = (lane64 >= 16 * h) & (lane64 < 16 * h + 16)
             a = dot(jnp.where(head, q64, 0.0).astype(BF16), qkT[64:, :]) * 0.25
             weight = jnp.where(allowed, 1.0 + a + 0.5 * a * a, 0.0).astype(BF16)
-            vh = v[:, 128 * h : 128 * h + 128]
+            vh = jnp.where(ones_row, 1.0, acc[128 * h + 128 : 128 * h + 256])
             state = run[h]
             s_hi = state.astype(BF16)
             s_lo = (state - s_hi.astype(F32)).astype(BF16)
             pqh = pq[:, 256 * h : 256 * h + 256]
             both = dot(pqh, jnp.concatenate([s_hi, s_lo], axis=1))
-            num[rows, 128 * h : 128 * h + 128] = dot(weight, vh.astype(BF16)) + from_top * (
+            num[rows, 128 * h : 128 * h + 128] = dot_nt(weight, vh.astype(BF16)) + from_top * (
                 both[:, :128] + both[:, 128:]
             )
             parts = []
             for j in range(ENDS):
-                mark = (slot_col == j) & (stops[j] <= T)
+                mark = (slot_row == j) & (stops[j] <= T)
                 parts.append(jnp.where(mark, vh, 0.0).astype(BF16))
-            parts.append(jnp.where(slot_col == slot_next, vh, 0.0).astype(BF16))
-            made = dot(pk[256 * h : 256 * h + 256, :], jnp.concatenate(parts, axis=1))
+            parts.append(jnp.where(slot_row == slot_next, vh, 0.0).astype(BF16))
+            made = dot_nt(pk[256 * h : 256 * h + 256, :], jnp.concatenate(parts, axis=0))
             eacc[h] += made[:ROWS, : ENDS * 128]
             run[h] = keep * state + made[:, ENDS * 128 :]
         return x
@@ -387,7 +391,7 @@
             got = dot(psiq[rows, 256 * h : 256 * h + 256], run[h].astype(BF16))
             both = num[rows, 128 * h : 128 * h + 128] + jnp.where(slot_col == 0, got, 0.0)
             parts.append((both / both[:, HV : HV + 1]).astype(BF16))
-        out[rows, :] = dot(jnp.concatenate(parts, axis=1), pack[...]).astype(BF16)
+        out[:, rows] = dot_nt(unpack[...], jnp.concatenate(parts, axis=1)).astype(BF16)
         return x
 
     lax.fori_loop(0, NC, close, 0)
@@ -395,8 +399,8 @@
     got = stage[...].astype(BF16)
     flag = resume[inv[me]].astype(F32)
     fstate[0] = flag * init[0] + spread_s[...] * dot(spread[...], dot(got, pack[...]).astype(BF16))
-    moved = spread_s[...] * dot(spread[...], dot(got, pack_n[...]).astype(BF16))
-    fnorm[0] = flag * norm[0] + moved[:, :HD]
+    moved = spread_t[...] * dot_nt(dot_nt(unpack_n[...], got).astype(BF16), spread[...])
+    fnorm[0] = flag * norm[0] + moved
 
     for c in range(NC):
         for way in (0, 1):
@@ -408,27 +412,29 @@
 
 def local(tokens, wq, wk, wv, lengths, owner, resume, init, norm):
     S, Z = lax.axis_size("seq"), lax.axis_size("tp")
-    T, FW = tokens.shape
+    tokens, norm = tokens.T, jnp.transpose(norm, (0, 2, 1))
+    FW, T = tokens.shape
     C = T // 6
     SR = HD * ROWS // S
     consts = tables(float(T * S // 2))
     smem = pl.BlockSpec(memory_space=pltpu.SMEM)
     vmem = pl.BlockSpec(memory_space=pltpu.VMEM)
     hbm = pl.BlockSpec(memory_space=pl.ANY)
-    return pl.pallas_call(
+    out, state, moved = pl.pallas_call(
         functools.partial(kernel, S, Z, C),
         out_shape=(
-            jax.ShapeDtypeStruct((T, HD * HV), BF16),
+            jax.ShapeDtypeStruct((HD * HV, T), BF16),
             jax.ShapeDtypeStruct(init.shape, F32),
             jax.ShapeDtypeStruct(norm.shape, F32),
         ),
         in_specs=[smem] * 3 + [hbm] + [vmem] * (5 + len(consts)),
         out_specs=(vmem, vmem, vmem),
         scratch_shapes=[
-            pltpu.VMEM((Z, T, FW), BF16),
+            pltpu.VMEM((Z, FW, T), BF16),
             pltpu.VMEM((wq.shape[0], 640), BF16),
             pltpu.VMEM((S, wq.shape[0], 640), BF16),
             pltpu.VMEM((S * wq.shape[0], 640), F32),
+            pltpu.VMEM((Z, 640, FW), BF16),
             pltpu.VMEM((ROWS, HD * 128), F32),
             pltpu.VMEM((S, SR, 128), BF16),
             pltpu.VMEM((S, SR, 128), BF16),
@@ -459,6 +465,7 @@
             collective_id=0, has_side_effects=True, vmem_limit_bytes=60 * 2**20
         ),
     )(lengths, owner, resume, tokens, wq, wk, wv, init, norm, *consts)
+    return out.T, state, jnp.transpose(moved, (0, 2, 1))
 
 
 def solution(mesh):

time: 115 us -> 117 us (1.017)
  Pallas kernels: 103 us -> 109 us
  local copies, waits for them, and re-layouts: 10.6 us -> 7.45 us
    pallas_call x1, Pallas kernels: 103 us -> 109 us  [local(): pl.pallas_call(functools.partial(kernel, S, Z, C), out_shape=(jax.ShapeDt...]
    pallas_call x3 -> x0, local copies, waits for them, and re-layouts: 4.66 us -> none  [local(): pl.pallas_call(functools.partial(kernel, S, Z, C), out_shape=(jax.ShapeDt...]
    unnamed x7 -> x6, local copies, waits for them, and re-layouts: 5.97 us -> 7.45 us
where the time goes in v2:
time: 117 us
  Pallas kernels  109 us (93%)
  local copies, waits for them, and re-layouts  7.45 us (6%)
    pallas_call x1, Pallas kernels, local(): pl.pallas_call(functools.partial(kernel, S, Z, C), out_shape=(jax.ShapeDt...  109 us
    unnamed x6, local copies, waits for them, and re-layouts  7.45 us

profile of v2, /device:TPU:5, one launch (start us, length us, event | category | flops | bytes accessed | tf_op | source)
XLA Modules:
  0.0 117.0 jit_solution(10034142651086738019)
XLA Ops:
  0.6 1.9 %copy.26.init = f32[1,273,448]{2,1,0:T(8,128)} copy(f32[1,273,448]{2,0,1:T(1,128)} %param.30) | data formatting | bytes 978432 | tf_op args[7]
  2.5 108.9 %shard_map.238 = (bf16[448,1536]{1,0:T(8,128)(2,1)}, f32[1,273,448]{2,1,0:T(8,128)}, f32[1,4,273]{2,1,0:T(4,128)}) custom-call(s32[32]{0:T(128)} %lengths.1, s32[32]{0:T(128)} %owner.1, s32[32]{0:T(128)} %resume.1, bf16[448,1536]{1,0:T(8,128)(2,1)} %bitcast.4, bf16[56,64]{1,0:T(8,128)(2,1)} %wq.1, bf16[56,64]{1,0:T(8,128)(2,1)} %wk.1, bf16[56,448]{1,0:T(8,128)(2,1)} %wv.1, ...), custom_call_target="tpu_custom_call" | custom-call | tf_op jit(solution)/shard_map/pallas_call | solution.py:423
  111.5 2.4 %copy.27 = f32[1,273,448]{2,0,1:T(1,128)} copy(f32[1,273,448]{2,1,0:T(8,128)} %get-tuple-element.10) | data formatting | bytes 978432
  113.9 0.0 copy-start
  113.9 2.5 %copy.30 = bf16[1536,448]{0,1:T(8,128)(2,1)} copy(bf16[1536,448]{0,1:T(8,128)(2,1)} %bitcast.5) | data formatting | bytes 2752512
  116.4 0.0 copy-done
  116.4 0.6 copy.31
Async XLA Ops:
  113.9 2.5 %copy-start = (f32[1,4,273]{2,1,0:T(4,128)S(1)}, f32[1,4,273]{2,1,0:T(4,128)}, u32[]{:S(2)}) copy-start(f32[1,4,273]{2,1,0:T(4,128)} %get-tuple-element.8) | copy-start | bytes 13108

commit v3 on v1

--- a/solution.py
+++ b/solution.py
@@ -82,20 +82,24 @@
     f32 = lambda x: jnp.asarray(x, F32)
     return (
         bf(q1), bf(q2), bf(k1), bf(k2), f32(bq), f32(bk), bf(fold), f32(fold_scale), bf(spread),
-        f32(spread_scale), bf(pack), bf(pack.T), bf(pack_n), bf(pack_n.T[:HD]),
+        f32(spread_scale), f32(spread_scale.T), bf(pack), bf(pack.T), bf(pack_n.T[:HD]),
     )
 
 
 def dot(a, b):
     return jnp.dot(a, b, preferred_element_type=F32)
+
+
+def dot_nt(a, b):
+    return lax.dot_general(a, b, (((1,), (1,)), ((), ())), preferred_element_type=F32)
 
 
 def kernel(
     S, Z, C,
     lengths, owner, resume, tokens, wq, wk, wv, init, norm,
-    q1, q2, k1, k2, bq, bk, fold, fold_s, spread, spread_s, pack, unpack, pack_n, unpack_n,
+    q1, q2, k1, k2, bq, bk, fold, fold_s, spread, spread_s, spread_t, pack, unpack, unpack_n,
     out, fstate, fnorm,
-    gat, wsend, wrecv, wall, stage, isend, irecv, ssend, srecv, start, lsend, lrecv, csend, crecv,
+    gat, wsend, wrecv, wall, wallb, stage, isend, irecv, ssend, srecv, start, lsend, lrecv, csend, crecv,
     psiq, num, eacc, run, ftab,
     ends, first, inv,
     own_sem, dsend, drecv, fsend, frecv, xsend, xrecv,
@@ -135,7 +139,7 @@
     full = norm[0]
     hi = full.astype(BF16)
     lo = (full - hi.astype(F32)).astype(BF16)
-    folded_n = (dot(fold[...], hi) + dot(fold[...], lo)) * fold_s[...]
+    folded_n = (dot_nt(fold[...], hi) + dot_nt(fold[...], lo)) * fold_s[...]
     stage[...] = dot(folded.astype(BF16), unpack[...]) + dot(folded_n.astype(BF16), unpack_n[...])
     for s in range(S):
         h, k = s // PH, s % PH
@@ -190,11 +194,51 @@
         part = buf.at[pl.ds(0, S - 1)]
         pltpu.make_async_copy(part, part, xsend.at[n]).wait()
 
+    side = lax.rem(me, 2)
+    twin = me + 1 - 2 * side
+
+    def spread_weights():
+        pltpu.make_async_copy(wsend, wrecv.at[me], xrecv.at[1]).start()
+
+        def send(i, x):
+            pltpu.make_async_remote_copy(
+                src_ref=wsend,
+                dst_ref=wrecv.at[me],
+                send_sem=xsend.at[1],
+                recv_sem=xrecv.at[1],
+                device_id={"seq": lax.rem(me + 2 * i, S)},
+                device_id_type=MESH,
+            ).start()
+            return x
+
+        lax.fori_loop(1, S // 2, send, 0)
+
+    def half_arrived(n):
+        part = wrecv.at[pl.ds(0, S // 2)]
+        pltpu.make_async_copy(part, part, xrecv.at[n]).wait()
+
+    def share_weights():
+        half_arrived(1)
+
+        def send(i, x):
+            place = wrecv.at[2 * i + side]
+            pltpu.make_async_remote_copy(
+                src_ref=place,
+                dst_ref=place,
+                send_sem=xsend.at[5],
+                recv_sem=xrecv.at[5],
+                device_id={"seq": twin},
+                device_id_type=MESH,
+            ).start()
+            return x
+
+        lax.fori_loop(0, S // 2, send, 0)
+
     for c in range(3):
         for way in (0, 1):
             direct(way, c).start()
+    spread_weights()
     exchange(lambda p: isend.at[p], lambda p: irecv.at[p], 0)
-    exchange(lambda p: wsend, lambda p: wrecv.at[p], 1)
 
     total = jnp.int32(0)
     for r in range(S):
@@ -225,7 +269,6 @@
         return x
 
     lax.fori_loop(0, S, pick, 0)
-    exchange(lambda p: ssend.at[p], lambda p: srecv.at[p], 2)
 
     def relay(c):
         for way in (0, 1):
@@ -249,14 +292,19 @@
             slot = slot + jnp.where(pos >= stop, 1, 0)
         return slot
 
-    for c in range(4):
+    for c in range(2):
+        relay(c)
+    share_weights()
+    exchange(lambda p: ssend.at[p], lambda p: srecv.at[p], 2)
+    for c in range(2, 4):
         relay(c)
 
     run[...] = jnp.zeros_like(run)
     eacc[...] = jnp.zeros_like(eacc)
-    arrived(wrecv, 1)
+    half_arrived(5)
     for s in range(S):
         wall[WR * s : WR * s + WR, :] = wrecv[s].astype(wall.dtype)
+    wallb[...] = wall[...].astype(BF16)
     own.wait()
 
     lane64 = lax.broadcasted_iota(jnp.int32, (1, 64), 1)
@@ -277,7 +325,7 @@
         rows = pl.ds(pl.multiple_of(c * C, C), C)
         acc = jnp.zeros((C, 640), F32)
         for z in range(Z):
-            acc = acc + dot(gat[z, rows, :], wall[z * FW : (z + 1) * FW, :].astype(BF16))
+            acc = acc + dot(gat[z, rows, :], wallb[z * FW : (z + 1) * FW, :])
         qk32 = acc[:, :128]
         qk = qk32.astype(BF16)
         v = jnp.where(ones_col, 1.0, acc[:, 128:].astype(BF16).astype(F32))
@@ -395,19 +443,23 @@
     got = stage[...].astype(BF16)
     flag = resume[inv[me]].astype(F32)
     fstate[0] = flag * init[0] + spread_s[...] * dot(spread[...], dot(got, pack[...]).astype(BF16))
-    moved = spread_s[...] * dot(spread[...], dot(got, pack_n[...]).astype(BF16))
-    fnorm[0] = flag * norm[0] + moved[:, :HD]
+    moved = spread_t[...] * dot_nt(dot_nt(unpack_n[...], got).astype(BF16), spread[...])
+    fnorm[0] = flag * norm[0] + moved
 
     for c in range(NC):
         for way in (0, 1):
             direct(way, c).wait_send()
             onward(way, c).wait_send()
-    for n, buf in ((0, isend), (1, wrecv), (2, ssend), (3, lsend), (4, csend)):
+    for n, buf in ((0, isend), (2, ssend), (3, lsend), (4, csend)):
         sent(buf, n)
+    for n, copies in ((1, S // 2 - 1), (5, S // 2)):
+        part = wrecv.at[pl.ds(0, copies)]
+        pltpu.make_async_copy(part, part, xsend.at[n]).wait()
 
 
 def local(tokens, wq, wk, wv, lengths, owner, resume, init, norm):
     S, Z = lax.axis_size("seq"), lax.axis_size("tp")
+    norm = jnp.transpose(norm, (0, 2, 1))
     T, FW = tokens.shape
     C = T // 6
     SR = HD * ROWS // S
@@ -415,7 +467,7 @@
     smem = pl.BlockSpec(memory_space=pltpu.SMEM)
     vmem = pl.BlockSpec(memory_space=pltpu.VMEM)
     hbm = pl.BlockSpec(memory_space=pl.ANY)
-    return pl.pallas_call(
+    out, state, moved = pl.pallas_call(
         functools.partial(kernel, S, Z, C),
         out_shape=(
             jax.ShapeDtypeStruct((T, HD * HV), BF16),
@@ -429,6 +481,7 @@
             pltpu.VMEM((wq.shape[0], 640), BF16),
             pltpu.VMEM((S, wq.shape[0], 640), BF16),
             pltpu.VMEM((S * wq.shape[0], 640), F32),
+            pltpu.VMEM((S * wq.shape[0], 640), BF16),
             pltpu.VMEM((ROWS, HD * 128), F32),
             pltpu.VMEM((S, SR, 128), BF16),
             pltpu.VMEM((S, SR, 128), BF16),
@@ -452,13 +505,14 @@
             pltpu.SemaphoreType.DMA((2, 6)),
             pltpu.SemaphoreType.DMA((2, 6)),
             pltpu.SemaphoreType.DMA((2, 6)),
-            pltpu.SemaphoreType.DMA((5,)),
-            pltpu.SemaphoreType.DMA((5,)),
+            pltpu.SemaphoreType.DMA((6,)),
+            pltpu.SemaphoreType.DMA((6,)),
         ],
         compiler_params=pltpu.CompilerParams(
             collective_id=0, has_side_effects=True, vmem_limit_bytes=60 * 2**20
         ),
     )(lengths, owner, resume, tokens, wq, wk, wv, init, norm, *consts)
+    return out, state, jnp.transpose(moved, (0, 2, 1))
 
 
 def solution(mesh):

time: 115 us -> 113 us (0.983)
  local copies, waits for them, and re-layouts: 10.6 us -> 9.02 us
    pallas_call x3 -> x0, local copies, waits for them, and re-layouts: 4.66 us -> none  [local(): pl.pallas_call(functools.partial(kernel, S, Z, C), out_shape=(jax.ShapeDt...]
    unnamed x7 -> x9, local copies, waits for them, and re-layouts: 5.97 us -> 9.02 us
where the time goes in v3:
time: 113 us; the launch traced here: 112 us
  Pallas kernels  103 us (91%)
  local copies, waits for them, and re-layouts  9.02 us (8%)
    pallas_call x1, Pallas kernels, local(): pl.pallas_call(functools.partial(kernel, S, Z, C), out_shape=(jax.ShapeDt...  103 us
    unnamed x9, local copies, waits for them, and re-layouts  9.02 us

profile of v3, /device:TPU:5, one launch (start us, length us, event | category | flops | bytes accessed | tf_op | source)
XLA Modules:
  0.0 112.5 jit_solution(2595068272130358735)
XLA Ops:
  0.6 1.9 %copy.27.init = f32[1,273,448]{2,1,0:T(8,128)} copy(f32[1,273,448]{2,0,1:T(1,128)} %param.30) | data formatting | bytes 978432 | tf_op args[7]
  2.5 2.6 %copy.26.tokens = bf16[1536,448]{1,0:T(8,128)(2,1)} copy(bf16[1536,448]{0,1:T(8,128)(2,1)} %param.23) | data formatting | bytes 2752512 | tf_op args[0]
  5.1 102.8 %shard_map.238 = (bf16[1536,448]{1,0:T(8,128)(2,1)}, f32[1,273,448]{2,1,0:T(8,128)}, f32[1,4,273]{2,1,0:T(4,128)}) custom-call(s32[32]{0:T(128)} %lengths.1, s32[32]{0:T(128)} %owner.1, s32[32]{0:T(128)} %resume.1, bf16[1536,448]{1,0:T(8,128)(2,1)} %copy.26.tokens, bf16[56,64]{1,0:T(8,128)(2,1)} %wq.1, bf16[56,64]{1,0:T(8,128)(2,1)} %wk.1, ...), custom_call_target="tpu_custom_call" | custom-call | tf_op jit(solution)/shard_map/pallas_call | solution.py:470
  107.9 0.0 copy-start
  107.9 0.0 copy-start.1
  107.9 2.6 %copy.28 = bf16[1536,448]{0,1:T(8,128)(2,1)} copy(bf16[1536,448]{1,0:T(8,128)(2,1)} %get-tuple-element.9) | data formatting | bytes 2752512
  110.5 0.0 copy-done
  110.5 1.4 %copy.29 = f32[1,273,448]{2,0,1:T(1,128)} copy(f32[1,273,448]{2,1,0:T(8,128)S(1)} %copy-done) | data formatting | bytes 978432
  111.9 0.0 copy-done.1
  111.9 0.6 copy.31
Async XLA Ops:
  107.9 2.6 %copy-start = (f32[1,273,448]{2,1,0:T(8,128)S(1)}, f32[1,273,448]{2,1,0:T(8,128)}, u32[]{:S(2)}) copy-start(f32[1,273,448]{2,1,0:T(8,128)} %get-tuple-element.10) | copy-start | bytes 1467652
  107.9 4.0 %copy-start.1 = (f32[1,4,273]{2,1,0:T(4,128)S(1)}, f32[1,4,273]{2,1,0:T(4,128)}, u32[]{:S(2)}) copy-start(f32[1,4,273]{2,1,0:T(4,128)} %get-tuple-element.8) | copy-start | bytes 13108
